TPU v7x, 32 devices: a whole 2x2x4 slice. The times are simulated.
32 devices in a mesh: grp: 2 (over x), chan: 16 (over z, y, core).
Axes of the slice: x: 2, y: 2, z: 4, core: 2. Of those that a mesh axis runs over, the one named last changes fastest.
Arguments:
- voltages: bfloat16 [8, 16384, 2048], P('grp', 'chan'), parts along dimension 0, may hold values from -6 to 6
- delay_step: int32 [16384], replicated, may hold values from 0 to 1048575
- trials: int32 [256], replicated, may hold values from 0 to 2047
Outputs:
- spectra: float32 [48, 2, 8, 256], P('chan', None, 'grp'), parts along dimension 2
- power: float32 [8, 256], P('grp', 'chan'), parts along dimension 0
There are 2 independent parts, one for each index of `grp`. A program takes and returns all parts, laid end to end along the dimension named above; an argument that names none is the same for every part. Nothing has to cross between parts.
All inputs are finite; a program needn't handle non-finite values.
Results may differ from a plain program's by a relative error of at most 0.0037.
Values may be sent and summed in bfloat16 or wider, within the bound.
No kernel may reach another device: no remote copies, remote signals or barrier semaphores. Data moves between devices by JAX's collectives and lax.ppermute only.
A program may use at most 64 MiB of HBM per device.

v0:
```python
import math
import jax
import jax.numpy as jnp
from jax import lax
from jax.sharding import PartitionSpec as P

SUBSTEPS = 512
SPIN_DEV = 3


def build_table(samples, bins):
    times = jnp.arange(samples, dtype=jnp.int32)
    frequency = jnp.arange(bins, dtype=jnp.int32)
    phase_index = times[:, None] * frequency[None, :] % samples
    angles = phase_index.astype(jnp.float32) * (2.0 * math.pi / samples)
    return jnp.concatenate([jnp.cos(angles), -jnp.sin(angles)], axis=1).astype(jnp.bfloat16)


def make_phases(spin_bin, delay_step, trials, modulus):
    chan_phase = spin_bin * delay_step % modulus
    phase_index = chan_phase[:, None] * trials[None, :] % modulus
    angles = phase_index.astype(jnp.float32) * (2.0 * math.pi / modulus)
    return jnp.concatenate([jnp.cos(angles), jnp.sin(angles)], axis=1)


def dedisperse(pair_rows, spin_bin, delay_step, trials, modulus, beam_count, chan_scale):
    rows_wide = pair_rows.astype(jnp.float32)
    half_count = trials.shape[0] // 2
    pieces = []
    for half_index in range(2):
        trial_half = trials[half_index * half_count : (half_index + 1) * half_count]
        phases = make_phases(spin_bin, delay_step, trial_half, modulus)
        product = jnp.dot(
            rows_wide, phases, precision=lax.Precision.HIGHEST, preferred_element_type=jnp.float32
        )
        real_rows = product[:beam_count]
        imag_rows = product[beam_count:]
        real_out = real_rows[:, :half_count] - imag_rows[:, half_count:]
        imag_out = real_rows[:, half_count:] + imag_rows[:, :half_count]
        pieces.append(jnp.stack([real_out, imag_out]))
    return jnp.concatenate(pieces, axis=2) * chan_scale


def per_device(voltages, delay_step, trials):
    beam_count, local_chan, samples = voltages.shape
    modulus = samples * SUBSTEPS
    chan_count = lax.axis_size("chan")
    bins_total = SPIN_DEV * chan_count
    all_chan = delay_step.shape[0]
    chan_scale = 1.0 / math.sqrt(all_chan)
    dft_table = build_table(samples, bins_total)
    spectrum = lax.dot_general(
        dft_table, voltages, (((0,), (2,)), ((), ())), preferred_element_type=jnp.float32
    )
    spectrum = (spectrum * (1.0 / math.sqrt(samples))).astype(jnp.bfloat16)
    spectrum = spectrum.reshape(2, bins_total, beam_count, local_chan)
    regrouped = lax.all_to_all(spectrum, "chan", split_axis=1, concat_axis=3, tiled=True)
    first_bin = lax.axis_index("chan") * SPIN_DEV

    def one_bin(offset):
        pair_rows = lax.dynamic_index_in_dim(regrouped, offset, axis=1, keepdims=False).reshape(
            2 * beam_count, all_chan
        )
        return dedisperse(
            pair_rows, first_bin + offset, delay_step, trials, modulus, beam_count, chan_scale
        )

    spectra = lax.map(one_bin, jnp.arange(SPIN_DEV, dtype=jnp.int32))
    power_part = jnp.sum(spectra * spectra, axis=(0, 1)) / bins_total
    power_out = lax.psum_scatter(power_part, "chan", scatter_dimension=1, tiled=True)
    return (spectra, power_out)


def solution(mesh):
    return jax.shard_map(
        per_device,
        mesh=mesh,
        in_specs=(P("grp", "chan", None), P(), P()),
        out_specs=(P("chan", None, "grp", None), P("grp", "chan")),
        check_vma=False,
    )
```

profile of v0, /device:TPU:0, one launch (start us, length us, event | category | flops | bytes accessed | tf_op | source)
XLA Modules:
  0.0 369.8 jit_solution(14272384766015729863)
XLA Ops:
  7.2 1.6 negate_convert_fusion
  8.8 11.1 %multiply_convert_fusion = bf16[96,4,1024]{2,0,1:T(8,128)(2,1)S(1)} fusion(bf16[4,1024,2048]{2,1,0:T(8,128)(2,1)} %param.5, bf16[2048,48]{0,1:T(8,128)(2,1)S(1)} %get-tuple-element.121, bf16[2048,48]{0,1:T(8,128)(2,1)S(1)} %get-tuple-element.122), kind=kOutput, calls=%fused_computation.47 | convolution fusion | flops 1612185600 | bytes 17956864 | tf_op jit(solution)/shard_map/dot_general | solution.py:52
  19.9 1.5 copy.9
  21.4 7.4 %all-to-all-start = ((bf16[2,48,4,1024]{3,2,0,1:T(4,128)(2,1)}), bf16[2,48,4,1024]{3,2,0,1:T(4,128)(2,1)S(1)}, u32[]{:S(2)}, u32[]{:S(2)}) async-start(bf16[2,48,4,1024]{3,2,0,1:T(4,128)(2,1)} %copy.9), calls=%async_computation | async-start | bytes 1572864 | tf_op jit(solution)/shard_map/all_to_all | solution.py:57
  28.8 0.0 reduce-scatter.4.cloned.1.call-start
  28.8 18.6 %all-to-all-done = bf16[2,48,4,1024]{3,2,0,1:T(4,128)(2,1)S(1)} async-done(((bf16[2,48,4,1024]{3,2,0,1:T(4,128)(2,1)}), bf16[2,48,4,1024]{3,2,0,1:T(4,128)(2,1)S(1)}, u32[]{:S(2)}, u32[]{:S(2)}) %all-to-all-start) | async-done | bytes 786464 | tf_op jit(solution)/shard_map/all_to_all | solution.py:57
  47.5 0.4 copy.11
  47.9 0.6 all_to_all.16
  48.5 256.2 %while.12 = (s32[]{:T(128)}, f32[3,2,4,256]{3,2,1,0:T(4,128)S(1)}, s32[3]{0:T(128)S(1)}, bf16[2,3,4,16384]{3,2,1,0:T(4,128)(2,1)S(1)}, s32[]{:T(128)}, /*index=5...) while((s32[]{:T(128)}, f32[3,2,4,256]{3,2,1,0:T(4,128)S(1)}, s32[3]{0:T(128)S(1)}, ...), condition=%wide.region_1.2_spmd, body=%wide.region_0.1_spmd.sunk | while | flops 872620032 | bytes 68955304 | solution.py:68
  48.7 0.6 dynamic_slice.18
  51.2 0.1 constant_dynamic-slice_fusion.2
  51.3 0.1 reshape.66
  52.1 67.4 %fusion.55 = (f32[16384,128]{1,0:T(8,128)S(1)}, f32[16384,128]{1,0:T(8,128)S(1)}, f32[16384,128]{1,0:T(8,128)}, f32[16384,128]{1,0:T(8,128)}) fusion(s32[128]{0:T(128)S(1)} %get-tuple-element.178, s32[16384]{0:T(1024)S(1)} %add_select_fusion.5, s32[128]{0:T(128)S(1)} %get-tuple-element.179), kind=kLoop, calls=%fused_computation.27.clone.1 | loop fusion | flops 58720256 | bytes 33620992 | tf_op jit(solution)/shard_map/while/body/eval_jaxpr/cos | solution.py:23
  119.5 8.9 %fusion.58 = f32[8,256]{1,0:T(8,128)S(1)} fusion(bf16[8,16384]{1,0:T(8,128)(2,1)S(1)} %reshape.66, f32[16384,128]{1,0:T(8,128)} %get-tuple-element.184, f32[16384,128]{1,0:T(8,128)} %get-tuple-element.185), kind=kOutput, calls=%fused_computation.4.clone.1 | convolution fusion | flops 406847488 | bytes 17047552 | tf_op jit(solution)/shard_map/while/body/eval_jaxpr/dot_general | solution.py:33
  128.5 5.5 %fusion.56 = f32[8,256]{1,0:T(8,128)S(1)} fusion(bf16[8,16384]{1,0:T(8,128)(2,1)S(1)} %reshape.66, f32[16384,128]{1,0:T(8,128)S(1)} %get-tuple-element.180, f32[16384,128]{1,0:T(8,128)S(1)} %get-tuple-element.181), kind=kOutput, calls=%fused_computation.clone.1 | convolution fusion | flops 406847488 | bytes 17047552 | tf_op jit(solution)/shard_map/while/body/eval_jaxpr/dot_general | solution.py:33
  134.1 0.6 dynamic_slice.18
  136.6 0.1 constant_dynamic-slice_fusion.2
  136.7 0.1 reshape.66
  137.4 67.4 %fusion.55 = (f32[16384,128]{1,0:T(8,128)S(1)}, f32[16384,128]{1,0:T(8,128)S(1)}, f32[16384,128]{1,0:T(8,128)}, f32[16384,128]{1,0:T(8,128)}) fusion(s32[128]{0:T(128)S(1)} %get-tuple-element.178, s32[16384]{0:T(1024)S(1)} %add_select_fusion.5, s32[128]{0:T(128)S(1)} %get-tuple-element.179), kind=kLoop, calls=%fused_computation.27.clone.1 | loop fusion | flops 58720256 | bytes 33620992 | tf_op jit(solution)/shard_map/while/body/eval_jaxpr/cos | solution.py:23
  204.9 8.9 %fusion.58 = f32[8,256]{1,0:T(8,128)S(1)} fusion(bf16[8,16384]{1,0:T(8,128)(2,1)S(1)} %reshape.66, f32[16384,128]{1,0:T(8,128)} %get-tuple-element.184, f32[16384,128]{1,0:T(8,128)} %get-tuple-element.185), kind=kOutput, calls=%fused_computation.4.clone.1 | convolution fusion | flops 406847488 | bytes 17047552 | tf_op jit(solution)/shard_map/while/body/eval_jaxpr/dot_general | solution.py:33
  213.8 5.5 %fusion.56 = f32[8,256]{1,0:T(8,128)S(1)} fusion(bf16[8,16384]{1,0:T(8,128)(2,1)S(1)} %reshape.66, f32[16384,128]{1,0:T(8,128)S(1)} %get-tuple-element.180, f32[16384,128]{1,0:T(8,128)S(1)} %get-tuple-element.181), kind=kOutput, calls=%fused_computation.clone.1 | convolution fusion | flops 406847488 | bytes 17047552 | tf_op jit(solution)/shard_map/while/body/eval_jaxpr/dot_general | solution.py:33
  219.4 0.6 dynamic_slice.18
  221.9 0.1 constant_dynamic-slice_fusion.2
  222.0 0.1 reshape.66
  222.8 67.4 %fusion.55 = (f32[16384,128]{1,0:T(8,128)S(1)}, f32[16384,128]{1,0:T(8,128)S(1)}, f32[16384,128]{1,0:T(8,128)}, f32[16384,128]{1,0:T(8,128)}) fusion(s32[128]{0:T(128)S(1)} %get-tuple-element.178, s32[16384]{0:T(1024)S(1)} %add_select_fusion.5, s32[128]{0:T(128)S(1)} %get-tuple-element.179), kind=kLoop, calls=%fused_computation.27.clone.1 | loop fusion | flops 58720256 | bytes 33620992 | tf_op jit(solution)/shard_map/while/body/eval_jaxpr/cos | solution.py:23
  290.2 8.9 %fusion.58 = f32[8,256]{1,0:T(8,128)S(1)} fusion(bf16[8,16384]{1,0:T(8,128)(2,1)S(1)} %reshape.66, f32[16384,128]{1,0:T(8,128)} %get-tuple-element.184, f32[16384,128]{1,0:T(8,128)} %get-tuple-element.185), kind=kOutput, calls=%fused_computation.4.clone.1 | convolution fusion | flops 406847488 | bytes 17047552 | tf_op jit(solution)/shard_map/while/body/eval_jaxpr/dot_general | solution.py:33
  299.1 5.5 %fusion.56 = f32[8,256]{1,0:T(8,128)S(1)} fusion(bf16[8,16384]{1,0:T(8,128)(2,1)S(1)} %reshape.66, f32[16384,128]{1,0:T(8,128)S(1)} %get-tuple-element.180, f32[16384,128]{1,0:T(8,128)S(1)} %get-tuple-element.181), kind=kOutput, calls=%fused_computation.clone.1 | convolution fusion | flops 406847488 | bytes 17047552 | tf_op jit(solution)/shard_map/while/body/eval_jaxpr/dot_general | solution.py:33
  304.7 0.0 copy-start.2
  304.8 0.8 copy.13
  305.6 0.0 reduce-scatter.4.cloned.1.call-update
  305.6 56.0 %reduce-scatter.4.cloned.1.call-done = f32[16,4]{1,0:T(8,128)} async-done(((f32[256,4]{1,0:T(8,128)}), f32[16,4]{1,0:T(8,128)}) %reduce-scatter.4.cloned.1.call-update) | async-done | bytes 272
  361.6 1.3 copy.14
  (27 shorter events, 0.3 us)
Async XLA Ops:
  8.8 39.7 %copy-start = (s32[16384]{0:T(1024)S(1)}, s32[16384]{0:T(1024)}, u32[]{:S(2)}) copy-start(s32[16384]{0:T(1024)} %param.6) | copy-start | bytes 196612
  8.8 39.7 %copy-start.1 = (s32[256]{0:T(256)S(1)}, s32[256]{0:T(256)}, u32[]{:S(2)}) copy-start(s32[256]{0:T(256)} %param.7) | copy-start | bytes 3076
  21.4 26.1 %all-to-all-start = ((bf16[2,48,4,1024]{3,2,0,1:T(4,128)(2,1)}), bf16[2,48,4,1024]{3,2,0,1:T(4,128)(2,1)S(1)}, u32[]{:S(2)}, u32[]{:S(2)}) async-start(bf16[2,48,4,1024]{3,2,0,1:T(4,128)(2,1)} %copy.9), calls=%async_computation | async-start | bytes 1572864 | tf_op jit(solution)/shard_map/all_to_all | solution.py:57
  28.8 332.8 %reduce-scatter.4.cloned.1.call-start = ((), (), s32[]{:S(2)}) async-start(), calls=%async_computation.2 | async-start | bytes 139264
  304.7 58.2 %copy-start.2 = (f32[3,2,4,256]{3,2,1,0:T(4,128)}, f32[3,2,4,256]{3,2,1,0:T(4,128)S(1)}, u32[]{:S(2)}) copy-start(f32[3,2,4,256]{3,2,1,0:T(4,128)S(1)} %get-tuple-element.90) | copy-start | bytes 73732
Sparse Core Ops, SparseCore 0:
  305.7 55.8 reduce-scatter.3
where the time goes:
time: 370 us
  other arithmetic  204 us (55%)
  waiting for transfers between devices  74.7 us (20%)
  matrix products  54.4 us (15%)
  between operations  14.1 us (4%)
  loops' own time  7.92 us (2%)
  starting transfers between devices  7.43 us (2%)
  local copies, waits for them, and re-layouts  7.09 us (2%)
    cos x3, other arithmetic, make_phases(): return jnp.concatenate([jnp.cos(angles), jnp.sin(angles)], axis=1)  202 us
    unnamed x2, waiting for transfers between devices  56 us
    dot_general x6, matrix products, dedisperse(): jnp.dot(rows_wide, phases, precision=lax.Precision.HIGHEST, preferred_ele...  43.3 us
    all_to_all x1, waiting for transfers between devices, per_device(): lax.all_to_all(spectrum, 'chan', split_axis=1, concat_axis=3, tiled=True)  18.6 us
    dot_general x1, matrix products, per_device(): lax.dot_general(dft_table, voltages, (((0,), (2,)), ((), ())), preferred_...  11.1 us
    another operation x1, loops' own time, per_device(): spectra = lax.map(one_bin, jnp.arange(SPIN_DEV, dtype=jnp.int32))  7.92 us
  transfers between devices with their start and end apart: 2, of which 2 were waited for; matrix products, arithmetic and copies ran while one was open for 0% of the time, Pallas kernels for 0%

commit v1 on v0

--- a/solution.py
+++ b/solution.py
@@ -54,7 +54,19 @@
     )
     spectrum = (spectrum * (1.0 / math.sqrt(samples))).astype(jnp.bfloat16)
     spectrum = spectrum.reshape(2, bins_total, beam_count, local_chan)
-    regrouped = lax.all_to_all(spectrum, "chan", split_axis=1, concat_axis=3, tiled=True)
+    ways, here = (lax.axis_size("chan"), lax.axis_index("chan"))
+    width = spectrum.shape[1] // ways
+    dims = list(spectrum.shape)
+    dims[1] = width
+    height = dims[3]
+    dims[3] = height * ways
+    full = jnp.zeros(dims, spectrum.dtype)
+    for mask in range(ways):
+        part = lax.dynamic_slice_in_dim(spectrum, (here ^ mask) * width, width, axis=1)
+        if mask:
+            part = lax.ppermute(part, "chan", [(d, d ^ mask) for d in range(ways)])
+        full = lax.dynamic_update_slice_in_dim(full, part, (here ^ mask) * height, axis=3)
+    regrouped = full
     first_bin = lax.axis_index("chan") * SPIN_DEV
 
     def one_bin(offset):

time: 370 us -> 373 us (level)
  starting transfers between devices: 7.43 us -> 23.2 us
  waiting for transfers between devices: 74.7 us -> 60.7 us
    ppermute x0 -> x15, starting transfers between devices: none -> 23.1 us  [per_device(): part = lax.ppermute(part, 'chan', [(d, d ^ mask) for d in range(ways)])]
    all_to_all x1 -> x0, waiting for transfers between devices: 18.6 us -> none  [per_device(): lax.all_to_all(spectrum, 'chan', split_axis=1, concat_axis=3, tiled=True)]
    all_to_all x1 -> x0, starting transfers between devices: 7.39 us -> none  [per_device(): lax.all_to_all(spectrum, 'chan', split_axis=1, concat_axis=3, tiled=True)]
    ppermute x0 -> x15, waiting for transfers between devices: none -> 6.09 us  [per_device(): part = lax.ppermute(part, 'chan', [(d, d ^ mask) for d in range(ways)])]
  transfers between devices with their start and end apart: 2 -> 16, of which waited for: 2 -> 4; matrix products, arithmetic and copies ran while one was open for 0% -> 0% of each run, Pallas kernels for 0% -> 0%
where the time goes in v1:
time: 373 us; the launch traced here: 372 us
  other arithmetic  204 us (55%)
  waiting for transfers between devices  60.7 us (16%)
  matrix products  54.4 us (15%)
  starting transfers between devices  23.2 us (6%)
  between operations  14.7 us (4%)
  loops' own time  7.88 us (2%)
  local copies, waits for them, and re-layouts  7.45 us (2%)
    cos x3, other arithmetic, make_phases(): return jnp.concatenate([jnp.cos(angles), jnp.sin(angles)], axis=1)  202 us
    unnamed x2, waiting for transfers between devices  54.6 us
    dot_general x6, matrix products, dedisperse(): jnp.dot(rows_wide, phases, precision=lax.Precision.HIGHEST, preferred_ele...  43.3 us
    ppermute x15, starting transfers between devices, per_device(): part = lax.ppermute(part, 'chan', [(d, d ^ mask) for d in range(ways)])  23.1 us
    dot_general x1, matrix products, per_device(): lax.dot_general(dft_table, voltages, (((0,), (2,)), ((), ())), preferred_...  11.1 us
    another operation x1, loops' own time, per_device(): spectra = lax.map(one_bin, jnp.arange(SPIN_DEV, dtype=jnp.int32))  7.88 us
  transfers between devices with their start and end apart: 16, of which 4 were waited for; matrix products, arithmetic and copies ran while one was open for 0% of the time, Pallas kernels for 0%

profile of v1, /device:TPU:0, one launch (start us, length us, event | category | flops | bytes accessed | tf_op | source)
XLA Modules:
  0.0 372.4 jit_solution(783669077388918906)
XLA Ops:
  7.3 1.6 negate_convert_fusion
  9.0 11.1 %multiply_convert_fusion = bf16[96,4,1024]{2,0,1:T(8,128)(2,1)S(1)} fusion(bf16[4,1024,2048]{2,1,0:T(8,128)(2,1)} %param.5, bf16[2048,48]{0,1:T(8,128)(2,1)S(1)} %get-tuple-element.137, bf16[2048,48]{0,1:T(8,128)(2,1)S(1)} %get-tuple-element.138), kind=kOutput, calls=%fused_computation.47 | convolution fusion | flops 1612185600 | bytes 17956864 | tf_op jit(solution)/shard_map/dot_general | solution.py:52
  20.1 1.4 constant_dynamic-slice_fusion.1
  21.5 0.5 collective-permute-start
  22.1 2.6 collective-permute-start.1
  25.0 1.8 collective-permute-start.3
  27.0 0.2 broadcast_in_dim.6
  28.0 2.7 collective-permute-start.5
  30.9 2.7 collective-permute-start.7
  33.8 3.5 collective-permute-start.9
  37.6 3.6 collective-permute-start.11
  41.4 4.4 %collective-permute-start.13 = (bf16[2,3,4,1024]{3,2,1,0:T(4,128)(2,1)S(1)}, bf16[2,3,4,1024]{3,2,1,0:T(4,128)(2,1)S(1)}, u32[]{:S(2)}, u32[]{:S(2)}) collective-permute-start(bf16[2,3,4,1024]{3,2,1,0:T(4,128)(2,1)S(1)} %copy.53), channel_id=1, source_target_pairs={{0,14},{1,15},{2,12},{3,13},{4,10},{5,11},{6,8},{7,9},{8,6},{9,7},... | collective-permute-start | bytes 147464 | tf_op jit(solution)/shard_map/ppermute | solution.py:67
  45.9 0.4 collective-permute-start.14
  46.4 0.7 collective-permute-done.12
  47.1 2.2 collective-permute-done.13
  49.3 3.2 collective-permute-done.14
  52.6 256.2 %while.12 = (s32[]{:T(128)}, f32[3,2,4,256]{3,2,1,0:T(4,128)S(1)}, s32[3]{0:T(128)S(1)}, bf16[2,3,4,16384]{3,2,1,0:T(4,128)(2,1)S(1)}, s32[]{:T(128)}, /*index=5...) while((s32[]{:T(128)}, f32[3,2,4,256]{3,2,1,0:T(4,128)S(1)}, s32[3]{0:T(128)S(1)}, ...), condition=%wide.region_1.2_spmd, body=%wide.region_0.1_spmd.sunk | while | flops 872620032 | bytes 68955304 | solution.py:80
  52.7 0.7 dynamic_slice.98
  56.1 67.4 %fusion.55 = (f32[16384,128]{1,0:T(8,128)S(1)}, f32[16384,128]{1,0:T(8,128)S(1)}, f32[16384,128]{1,0:T(8,128)}, f32[16384,128]{1,0:T(8,128)}) fusion(s32[128]{0:T(128)S(1)} %get-tuple-element.194, s32[16384]{0:T(1024)S(1)} %add_select_fusion.5, s32[128]{0:T(128)S(1)} %get-tuple-element.195), kind=kLoop, calls=%fused_computation.27.clone.1 | loop fusion | flops 58720256 | bytes 33620992 | tf_op jit(solution)/shard_map/while/body/eval_jaxpr/cos | solution.py:23
  123.6 8.9 %fusion.58 = f32[8,256]{1,0:T(8,128)S(1)} fusion(bf16[8,16384]{1,0:T(8,128)(2,1)S(1)} %reshape.66, f32[16384,128]{1,0:T(8,128)} %get-tuple-element.200, f32[16384,128]{1,0:T(8,128)} %get-tuple-element.201), kind=kOutput, calls=%fused_computation.4.clone.1 | convolution fusion | flops 406847488 | bytes 17047552 | tf_op jit(solution)/shard_map/while/body/eval_jaxpr/dot_general | solution.py:33
  132.5 5.5 %fusion.56 = f32[8,256]{1,0:T(8,128)S(1)} fusion(bf16[8,16384]{1,0:T(8,128)(2,1)S(1)} %reshape.66, f32[16384,128]{1,0:T(8,128)S(1)} %get-tuple-element.196, f32[16384,128]{1,0:T(8,128)S(1)} %get-tuple-element.197), kind=kOutput, calls=%fused_computation.clone.1 | convolution fusion | flops 406847488 | bytes 17047552 | tf_op jit(solution)/shard_map/while/body/eval_jaxpr/dot_general | solution.py:33
  138.1 0.7 dynamic_slice.98
  141.5 67.4 %fusion.55 = (f32[16384,128]{1,0:T(8,128)S(1)}, f32[16384,128]{1,0:T(8,128)S(1)}, f32[16384,128]{1,0:T(8,128)}, f32[16384,128]{1,0:T(8,128)}) fusion(s32[128]{0:T(128)S(1)} %get-tuple-element.194, s32[16384]{0:T(1024)S(1)} %add_select_fusion.5, s32[128]{0:T(128)S(1)} %get-tuple-element.195), kind=kLoop, calls=%fused_computation.27.clone.1 | loop fusion | flops 58720256 | bytes 33620992 | tf_op jit(solution)/shard_map/while/body/eval_jaxpr/cos | solution.py:23
  208.9 8.9 %fusion.58 = f32[8,256]{1,0:T(8,128)S(1)} fusion(bf16[8,16384]{1,0:T(8,128)(2,1)S(1)} %reshape.66, f32[16384,128]{1,0:T(8,128)} %get-tuple-element.200, f32[16384,128]{1,0:T(8,128)} %get-tuple-element.201), kind=kOutput, calls=%fused_computation.4.clone.1 | convolution fusion | flops 406847488 | bytes 17047552 | tf_op jit(solution)/shard_map/while/body/eval_jaxpr/dot_general | solution.py:33
  217.8 5.5 %fusion.56 = f32[8,256]{1,0:T(8,128)S(1)} fusion(bf16[8,16384]{1,0:T(8,128)(2,1)S(1)} %reshape.66, f32[16384,128]{1,0:T(8,128)S(1)} %get-tuple-element.196, f32[16384,128]{1,0:T(8,128)S(1)} %get-tuple-element.197), kind=kOutput, calls=%fused_computation.clone.1 | convolution fusion | flops 406847488 | bytes 17047552 | tf_op jit(solution)/shard_map/while/body/eval_jaxpr/dot_general | solution.py:33
  223.4 0.7 dynamic_slice.98
  226.8 67.4 %fusion.55 = (f32[16384,128]{1,0:T(8,128)S(1)}, f32[16384,128]{1,0:T(8,128)S(1)}, f32[16384,128]{1,0:T(8,128)}, f32[16384,128]{1,0:T(8,128)}) fusion(s32[128]{0:T(128)S(1)} %get-tuple-element.194, s32[16384]{0:T(1024)S(1)} %add_select_fusion.5, s32[128]{0:T(128)S(1)} %get-tuple-element.195), kind=kLoop, calls=%fused_computation.27.clone.1 | loop fusion | flops 58720256 | bytes 33620992 | tf_op jit(solution)/shard_map/while/body/eval_jaxpr/cos | solution.py:23
  294.3 8.9 %fusion.58 = f32[8,256]{1,0:T(8,128)S(1)} fusion(bf16[8,16384]{1,0:T(8,128)(2,1)S(1)} %reshape.66, f32[16384,128]{1,0:T(8,128)} %get-tuple-element.200, f32[16384,128]{1,0:T(8,128)} %get-tuple-element.201), kind=kOutput, calls=%fused_computation.4.clone.1 | convolution fusion | flops 406847488 | bytes 17047552 | tf_op jit(solution)/shard_map/while/body/eval_jaxpr/dot_general | solution.py:33
  303.2 5.5 %fusion.56 = f32[8,256]{1,0:T(8,128)S(1)} fusion(bf16[8,16384]{1,0:T(8,128)(2,1)S(1)} %reshape.66, f32[16384,128]{1,0:T(8,128)S(1)} %get-tuple-element.196, f32[16384,128]{1,0:T(8,128)S(1)} %get-tuple-element.197), kind=kOutput, calls=%fused_computation.clone.1 | convolution fusion | flops 406847488 | bytes 17047552 | tf_op jit(solution)/shard_map/while/body/eval_jaxpr/dot_general | solution.py:33
  308.8 0.8 copy.37
  309.6 54.6 %reduce-scatter.4.cloned.1.call-done = f32[16,4]{1,0:T(8,128)} async-done(((f32[256,4]{1,0:T(8,128)}), f32[16,4]{1,0:T(8,128)}) %reduce-scatter.4.cloned.1.call-update) | async-done | bytes 272
  364.2 1.3 copy.38
  (85 shorter events, 2.9 us)
Async XLA Ops:
  7.2 357.1 %reduce-scatter.4.cloned.1.call-start = ((), (), s32[]{:S(2)}) async-start(), calls=%async_computation.1 | async-start | bytes 139264
  9.0 43.5 %copy-start = (s32[16384]{0:T(1024)S(1)}, s32[16384]{0:T(1024)}, u32[]{:S(2)}) copy-start(s32[16384]{0:T(1024)} %param.6) | copy-start | bytes 196612
  9.0 43.5 %copy-start.1 = (s32[256]{0:T(256)S(1)}, s32[256]{0:T(256)}, u32[]{:S(2)}) copy-start(s32[256]{0:T(256)} %param.7) | copy-start | bytes 3076
  21.5 6.4 %collective-permute-start = (bf16[2,3,4,1024]{3,2,1,0:T(4,128)(2,1)S(1)}, bf16[2,3,4,1024]{3,2,1,0:T(4,128)(2,1)S(1)}, u32[]{:S(2)}, u32[]{:S(2)}) collective-permute-start(bf16[2,3,4,1024]{3,2,1,0:T(4,128)(2,1)S(1)} %copy.40), channel_id=1, source_target_pairs={{0,1},{1,0},{2,3},{3,2},{4,5},{5,4},{6,7},{7,6},{8,9},{9,8},{10,11... | collective-permute-start | bytes 147464 | tf_op jit(solution)/shard_map/ppermute | solution.py:67
  22.1 8.6 %collective-permute-start.1 = (bf16[2,3,4,1024]{3,2,1,0:T(4,128)(2,1)S(1)}, bf16[2,3,4,1024]{3,2,1,0:T(4,128)(2,1)S(1)}, u32[]{:S(2)}, u32[]{:S(2)}) collective-permute-start(bf16[2,3,4,1024]{3,2,1,0:T(4,128)(2,1)S(1)} %copy.41), channel_id=1, source_target_pairs={{0,2},{1,3},{2,0},{3,1},{4,6},{5,7},{6,4},{7,5},{8,10},{9,11},{10,... | collective-permute-start | bytes 147464 | tf_op jit(solution)/shard_map/ppermute | solution.py:67
  24.7 6.1 %collective-permute-start.2 = (bf16[2,3,4,1024]{3,2,1,0:T(4,128)(2,1)S(1)}, bf16[2,3,4,1024]{3,2,1,0:T(4,128)(2,1)S(1)}, u32[]{:S(2)}, u32[]{:S(2)}) collective-permute-start(bf16[2,3,4,1024]{3,2,1,0:T(4,128)(2,1)S(1)} %copy.42), channel_id=1, source_target_pairs={{0,3},{1,2},{2,1},{3,0},{4,7},{5,6},{6,5},{7,4},{8,11},{9,10},{10,... | collective-permute-start | bytes 147464 | tf_op jit(solution)/shard_map/ppermute | solution.py:67
  25.0 8.7 %collective-permute-start.3 = (bf16[2,3,4,1024]{3,2,1,0:T(4,128)(2,1)S(1)}, bf16[2,3,4,1024]{3,2,1,0:T(4,128)(2,1)S(1)}, u32[]{:S(2)}, u32[]{:S(2)}) collective-permute-start(bf16[2,3,4,1024]{3,2,1,0:T(4,128)(2,1)S(1)} %copy.43), channel_id=1, source_target_pairs={{0,4},{1,5},{2,6},{3,7},{4,0},{5,1},{6,2},{7,3},{8,12},{9,13},{10,... | collective-permute-start | bytes 147464 | tf_op jit(solution)/shard_map/ppermute | solution.py:67
  26.9 6.9 %collective-permute-start.4 = (bf16[2,3,4,1024]{3,2,1,0:T(4,128)(2,1)S(1)}, bf16[2,3,4,1024]{3,2,1,0:T(4,128)(2,1)S(1)}, u32[]{:S(2)}, u32[]{:S(2)}) collective-permute-start(bf16[2,3,4,1024]{3,2,1,0:T(4,128)(2,1)S(1)} %copy.44), channel_id=1, source_target_pairs={{0,5},{1,4},{2,7},{3,6},{4,1},{5,0},{6,3},{7,2},{8,13},{9,12},{10,... | collective-permute-start | bytes 147464 | tf_op jit(solution)/shard_map/ppermute | solution.py:67
  28.0 9.4 %collective-permute-start.5 = (bf16[2,3,4,1024]{3,2,1,0:T(4,128)(2,1)S(1)}, bf16[2,3,4,1024]{3,2,1,0:T(4,128)(2,1)S(1)}, u32[]{:S(2)}, u32[]{:S(2)}) collective-permute-start(bf16[2,3,4,1024]{3,2,1,0:T(4,128)(2,1)S(1)} %copy.45), channel_id=1, source_target_pairs={{0,6},{1,7},{2,4},{3,5},{4,2},{5,3},{6,0},{7,1},{8,14},{9,15},{10,... | collective-permute-start | bytes 147464 | tf_op jit(solution)/shard_map/ppermute | solution.py:67
  30.7 6.9 %collective-permute-start.6 = (bf16[2,3,4,1024]{3,2,1,0:T(4,128)(2,1)S(1)}, bf16[2,3,4,1024]{3,2,1,0:T(4,128)(2,1)S(1)}, u32[]{:S(2)}, u32[]{:S(2)}) collective-permute-start(bf16[2,3,4,1024]{3,2,1,0:T(4,128)(2,1)S(1)} %copy.46), channel_id=1, source_target_pairs={{0,7},{1,6},{2,5},{3,4},{4,3},{5,2},{6,1},{7,0},{8,15},{9,14},{10,... | collective-permute-start | bytes 147464 | tf_op jit(solution)/shard_map/ppermute | solution.py:67
  30.9 10.4 %collective-permute-start.7 = (bf16[2,3,4,1024]{3,2,1,0:T(4,128)(2,1)S(1)}, bf16[2,3,4,1024]{3,2,1,0:T(4,128)(2,1)S(1)}, u32[]{:S(2)}, u32[]{:S(2)}) collective-permute-start(bf16[2,3,4,1024]{3,2,1,0:T(4,128)(2,1)S(1)} %copy.47), channel_id=1, source_target_pairs={{0,8},{1,9},{2,10},{3,11},{4,12},{5,13},{6,14},{7,15},{8,0},{9,1},... | collective-permute-start | bytes 147464 | tf_op jit(solution)/shard_map/ppermute | solution.py:67
  33.7 7.7 %collective-permute-start.8 = (bf16[2,3,4,1024]{3,2,1,0:T(4,128)(2,1)S(1)}, bf16[2,3,4,1024]{3,2,1,0:T(4,128)(2,1)S(1)}, u32[]{:S(2)}, u32[]{:S(2)}) collective-permute-start(bf16[2,3,4,1024]{3,2,1,0:T(4,128)(2,1)S(1)} %copy.48), channel_id=1, source_target_pairs={{0,9},{1,8},{2,11},{3,10},{4,13},{5,12},{6,15},{7,14},{8,1},{9,0},... | collective-permute-start | bytes 147464 | tf_op jit(solution)/shard_map/ppermute | solution.py:67
  33.8 12.1 %collective-permute-start.9 = (bf16[2,3,4,1024]{3,2,1,0:T(4,128)(2,1)S(1)}, bf16[2,3,4,1024]{3,2,1,0:T(4,128)(2,1)S(1)}, u32[]{:S(2)}, u32[]{:S(2)}) collective-permute-start(bf16[2,3,4,1024]{3,2,1,0:T(4,128)(2,1)S(1)} %copy.49), channel_id=1, source_target_pairs={{0,10},{1,11},{2,8},{3,9},{4,14},{5,15},{6,12},{7,13},{8,2},{9,3},... | collective-permute-start | bytes 147464 | tf_op jit(solution)/shard_map/ppermute | solution.py:67
  37.4 8.9 %collective-permute-start.10 = (bf16[2,3,4,1024]{3,2,1,0:T(4,128)(2,1)S(1)}, bf16[2,3,4,1024]{3,2,1,0:T(4,128)(2,1)S(1)}, u32[]{:S(2)}, u32[]{:S(2)}) collective-permute-start(bf16[2,3,4,1024]{3,2,1,0:T(4,128)(2,1)S(1)} %copy.50), channel_id=1, source_target_pairs={{0,11},{1,10},{2,9},{3,8},{4,15},{5,14},{6,13},{7,12},{8,3},{9,2},... | collective-permute-start | bytes 147464 | tf_op jit(solution)/shard_map/ppermute | solution.py:67
  37.6 8.7 %collective-permute-start.11 = (bf16[2,3,4,1024]{3,2,1,0:T(4,128)(2,1)S(1)}, bf16[2,3,4,1024]{3,2,1,0:T(4,128)(2,1)S(1)}, u32[]{:S(2)}, u32[]{:S(2)}) collective-permute-start(bf16[2,3,4,1024]{3,2,1,0:T(4,128)(2,1)S(1)} %copy.51), channel_id=1, source_target_pairs={{0,12},{1,13},{2,14},{3,15},{4,8},{5,9},{6,10},{7,11},{8,4},{9,5},... | collective-permute-start | bytes 147464 | tf_op jit(solution)/shard_map/ppermute | solution.py:67
  41.3 5.8 %collective-permute-start.12 = (bf16[2,3,4,1024]{3,2,1,0:T(4,128)(2,1)S(1)}, bf16[2,3,4,1024]{3,2,1,0:T(4,128)(2,1)S(1)}, u32[]{:S(2)}, u32[]{:S(2)}) collective-permute-start(bf16[2,3,4,1024]{3,2,1,0:T(4,128)(2,1)S(1)} %copy.52), channel_id=1, source_target_pairs={{0,13},{1,12},{2,15},{3,14},{4,9},{5,8},{6,11},{7,10},{8,5},{9,4},... | collective-permute-start | bytes 147464 | tf_op jit(solution)/shard_map/ppermute | solution.py:67
  41.4 7.9 %collective-permute-start.13 = (bf16[2,3,4,1024]{3,2,1,0:T(4,128)(2,1)S(1)}, bf16[2,3,4,1024]{3,2,1,0:T(4,128)(2,1)S(1)}, u32[]{:S(2)}, u32[]{:S(2)}) collective-permute-start(bf16[2,3,4,1024]{3,2,1,0:T(4,128)(2,1)S(1)} %copy.53), channel_id=1, source_target_pairs={{0,14},{1,15},{2,12},{3,13},{4,10},{5,11},{6,8},{7,9},{8,6},{9,7},... | collective-permute-start | bytes 147464 | tf_op jit(solution)/shard_map/ppermute | solution.py:67
  45.9 6.6 %collective-permute-start.14 = (bf16[2,3,4,1024]{3,2,1,0:T(4,128)(2,1)S(1)}, bf16[2,3,4,1024]{3,2,1,0:T(4,128)(2,1)S(1)}, u32[]{:S(2)}, u32[]{:S(2)}) collective-permute-start(bf16[2,3,4,1024]{3,2,1,0:T(4,128)(2,1)S(1)} %copy.54), channel_id=1, source_target_pairs={{0,15},{1,14},{2,13},{3,12},{4,11},{5,10},{6,9},{7,8},{8,7},{9,6},... | collective-permute-start | bytes 147464 | tf_op jit(solution)/shard_map/ppermute | solution.py:67
  308.8 56.8 %copy-start.2 = (f32[3,2,4,256]{3,2,1,0:T(4,128)}, f32[3,2,4,256]{3,2,1,0:T(4,128)S(1)}, u32[]{:S(2)}) copy-start(f32[3,2,4,256]{3,2,1,0:T(4,128)S(1)} %get-tuple-element.90) | copy-start | bytes 73732
Sparse Core Ops, SparseCore 0:
  309.8 54.4 reduce-scatter.3
